TPU v7x, 32 devices: a whole 2x2x4 slice. The times are simulated.
32 devices in a mesh: space: 16 (over z, x, core), tm: 2 (over y).
Axes of the slice: x: 2, y: 2, z: 4, core: 2. Of those that a mesh axis runs over, the one named last changes fastest.
Arguments:
- node_feats: bfloat16 [128, 7168, 128], P('tm', 'space'), may hold values from -6 to 6
- positions: float32 [128, 3, 7168], P('tm', None, 'space'), may hold values from -3 to 3
- neighbours: int32 [128, 224, 8], P('tm', 'space'), may hold values from 0 to 223, as said below
- edge_in: bfloat16 [256, 128], replicated, may hold values from -0.375 to 0.375
- edge_out: bfloat16 [128, 128], replicated, may hold values from -0.5 to 0.5
- edge_params: float32 [3, 128], replicated, may hold values from -3 to 3
- coord_weight: float32 [128], replicated, may hold values from -0.5 to 0.5
- spectral: bfloat16 [2, 64, 128, 128], replicated, may hold values from -0.375 to 0.375
- node_in: bfloat16 [256, 128], replicated, may hold values from -0.375 to 0.375
- node_out: bfloat16 [128, 128], replicated, may hold values from -0.5 to 0.5
- node_bias: float32 [2, 128], replicated, may hold values from -3 to 3
Outputs:
- new_feats: bfloat16 [128, 7168, 128], P('tm', 'space')
- new_positions: float32 [128, 3, 7168], P('tm', None, 'space')
Inputs may be any that keep to these rules, and one draw needn't show every extreme that they name: neighbours[f, b, s] = (b + o) mod 224 for an offset o with -6 <= o <= 6; the offsets of a block's list may repeat, and every list holds the offsets 0, -6 and +6 in some slots.
All inputs are finite; a program needn't handle non-finite values.
Results may differ from a plain program's by a relative error of at most 0.0065.
Values may be sent and summed in bfloat16 or wider, within the bound.
No kernel may reach another device: no remote copies, remote signals or barrier semaphores. Data moves between devices by JAX's collectives and lax.ppermute only.
A program may use at most 320 MiB of HBM per device.

v0:
```python
import math

import jax
import jax.numpy as jnp
from jax import lax
from jax.sharding import PartitionSpec as P

BLOCK = 32
GHOST = 6


def with_halo(block, sides, width):
    for axis, dim in sides:
        count = lax.axis_size(axis)
        forward = [(i, i + 1) for i in range(count - 1)]
        forward.append((count - 1, 0))
        backward = [(target, source) for source, target in forward]
        low = lax.ppermute(
            lax.slice_in_dim(block, block.shape[dim] - width, None, axis=dim), axis, forward
        )
        high = lax.ppermute(lax.slice_in_dim(block, 0, width, axis=dim), axis, backward)
        block = jnp.concatenate([low, block, high], axis=dim)
    return block


def split_parts(values):
    high_part = values.astype(jnp.bfloat16)
    low_part = (values - high_part.astype(jnp.float32)).astype(jnp.bfloat16)
    return (high_part, low_part)


def edge_pass(own_src, other_dst, own_pos, other_pos, picked, edge_out, edge_params, coord_weight):
    frames, own_blocks, block_len, feat_width = own_src.shape
    other_blocks = other_dst.shape[1]
    flat_dst = other_dst.reshape(frames, other_blocks, block_len * feat_width)
    dst_high, dst_low = split_parts(flat_dst)
    block_ids = jnp.arange(other_blocks, dtype=jnp.int32)
    summed = jnp.zeros(own_src.shape, jnp.float32)
    moved = jnp.zeros(own_pos.shape, jnp.float32)
    for slot_num in range(picked.shape[2]):
        chosen = picked[:, :, slot_num]
        select_f32 = (chosen[:, :, None] == block_ids[None, None, :]).astype(jnp.float32)
        select_bf = select_f32.astype(jnp.bfloat16)
        near_dst = jnp.einsum(
            "fbc,fcx->fbx", select_bf, dst_high, preferred_element_type=jnp.float32
        ) + jnp.einsum("fbc,fcx->fbx", select_bf, dst_low, preferred_element_type=jnp.float32)
        near_dst = near_dst.reshape(own_src.shape)
        near_pos = jnp.einsum(
            "fbc,fdcl->fdbl", select_f32, other_pos, precision=lax.Precision.HIGHEST
        )
        offset_vec = own_pos - near_pos
        dist_sq = jnp.sum(offset_vec * offset_vec, axis=1)
        pre_act = own_src + near_dst + edge_params[0] + dist_sq[..., None] * edge_params[1]
        hidden = jax.nn.silu(pre_act).astype(jnp.bfloat16)
        out_act = (
            jnp.dot(
                hidden.reshape(-1, feat_width), edge_out, preferred_element_type=jnp.float32
            ).reshape(pre_act.shape)
            + edge_params[2]
        )
        message = jax.nn.silu(out_act)
        summed = summed + message
        weight = jnp.sum(message * coord_weight, axis=-1) / (1.0 + jnp.sqrt(dist_sq + 1.0))
        moved = moved + offset_vec * weight[:, None]
    return (summed, moved)


def spectral_conv(msg_block, spectral, out_count):
    frame_count, item_count, feat_width = msg_block.shape
    mode_count = spectral.shape[1]
    mode_ids = jnp.arange(mode_count, dtype=jnp.int32)
    time_ids = jnp.arange(frame_count, dtype=jnp.int32)
    step_angle = 2.0 * math.pi / frame_count
    angles = (mode_ids[:, None] * time_ids[None, :] % frame_count).astype(jnp.float32) * step_angle
    forward = jnp.concatenate([jnp.cos(angles), -jnp.sin(angles)], axis=0)
    fwd_high, fwd_low = split_parts(forward)
    flat_msg = msg_block.reshape(frame_count, -1)
    coeffs = jnp.dot(fwd_high, flat_msg, preferred_element_type=jnp.float32) + jnp.dot(
        fwd_low, flat_msg, preferred_element_type=jnp.float32
    )
    coeffs = coeffs.astype(jnp.bfloat16).reshape(2, mode_count, item_count, feat_width)
    mixed_real = jnp.einsum(
        "knh,khg->kng", coeffs[0], spectral[0], preferred_element_type=jnp.float32
    ) - jnp.einsum("knh,khg->kng", coeffs[1], spectral[1], preferred_element_type=jnp.float32)
    mixed_imag = jnp.einsum(
        "knh,khg->kng", coeffs[0], spectral[1], preferred_element_type=jnp.float32
    ) + jnp.einsum("knh,khg->kng", coeffs[1], spectral[0], preferred_element_type=jnp.float32)
    out_times = jnp.arange(out_count, dtype=jnp.int32)
    back_angles = (out_times[:, None] * mode_ids[None, :] % frame_count).astype(
        jnp.float32
    ) * step_angle
    weights = (jnp.where(mode_ids == 0, 1.0, 2.0) / frame_count).astype(jnp.float32)
    inverse = jnp.concatenate(
        [jnp.cos(back_angles) * weights, -jnp.sin(back_angles) * weights], axis=1
    )
    inv_high, inv_low = split_parts(inverse)
    mixed_all = jnp.concatenate([mixed_real, mixed_imag], axis=0).reshape(2 * mode_count, -1)
    mix_high, mix_low = split_parts(mixed_all)
    conv_out = (
        jnp.dot(inv_high, mix_high, preferred_element_type=jnp.float32)
        + jnp.dot(inv_low, mix_high, preferred_element_type=jnp.float32)
        + jnp.dot(inv_high, mix_low, preferred_element_type=jnp.float32)
    )
    return conv_out.astype(jnp.bfloat16).reshape(out_count, item_count, feat_width)


def shards(
    node_feats,
    positions,
    neighbours,
    edge_in,
    edge_out,
    edge_params,
    coord_weight,
    spectral,
    node_in,
    node_out,
    node_bias,
):
    frames, local_rows, feat_width = node_feats.shape
    blocks = local_rows // BLOCK
    rim_rows = GHOST * BLOCK
    slot_count = neighbours.shape[2]
    slab_index = lax.axis_index("space")
    total_blocks = blocks * lax.axis_size("space")
    first_block = slab_index * blocks - GHOST
    ext_feats = with_halo(node_feats, (("space", 1),), rim_rows)
    ext_pos = with_halo(positions.astype(jnp.bfloat16), (("space", 2),), rim_rows).astype(
        positions.dtype
    )
    ext_pos4 = ext_pos.reshape(frames, 3, blocks + 2 * GHOST, BLOCK)
    own_src = jnp.dot(node_feats, edge_in[:feat_width], preferred_element_type=jnp.float32).reshape(
        frames, blocks, BLOCK, feat_width
    )
    own_pos = positions.reshape(frames, 3, blocks, BLOCK)
    picked = (neighbours - first_block) % total_blocks
    ext_dst = jnp.dot(ext_feats, edge_in[feat_width:], preferred_element_type=jnp.float32).reshape(
        frames, blocks + 2 * GHOST, BLOCK, feat_width
    )
    summed, moved = edge_pass(
        own_src, ext_dst, own_pos, ext_pos4, picked, edge_out, edge_params, coord_weight
    )
    mean_msg = (summed / slot_count).astype(jnp.bfloat16).reshape(frames, local_rows, feat_width)
    new_positions = positions + (moved / slot_count).reshape(frames, 3, local_rows)
    regrouped = lax.all_to_all(mean_msg, "tm", split_axis=1, concat_axis=0, tiled=True)
    conv_all = spectral_conv(regrouped, spectral, regrouped.shape[0])
    conv_own = lax.all_to_all(conv_all, "tm", split_axis=0, concat_axis=1, tiled=True)
    node_pre = (
        jnp.dot(node_feats, node_in[:feat_width], preferred_element_type=jnp.float32)
        + jnp.dot(conv_own, node_in[feat_width:], preferred_element_type=jnp.float32)
        + node_bias[0]
    )
    node_hidden = jax.nn.silu(node_pre).astype(jnp.bfloat16)
    new_feats = (
        node_feats.astype(jnp.float32)
        + (jnp.dot(node_hidden, node_out, preferred_element_type=jnp.float32) + node_bias[1])
    ).astype(jnp.bfloat16)
    return (new_feats, new_positions)


def solution(mesh):
    placed = (
        P("tm", "space", None),
        P("tm", None, "space"),
        P("tm", "space", None),
        P(),
        P(),
        P(),
        P(),
        P(),
        P(),
        P(),
        P(),
    )
    return jax.shard_map(
        shards,
        mesh=mesh,
        in_specs=placed,
        out_specs=(P("tm", "space", None), P("tm", None, "space")),
        check_vma=False,
    )
```

profile of v0, /device:TPU:1, one launch (start us, length us, event | category | flops | bytes accessed | tf_op | source)
XLA Modules:
  0.0 959.1 jit_solution(7866914278327090848)
XLA Ops:
  14.3 10.3 %fusion.99 = f32[64,448,128]{2,1,0:T(8,128)} fusion(bf16[64,448,128]{2,1,0:T(8,128)(2,1)} %param.11, bf16[256,128]{1,0:T(8,128)(2,1)S(1)} %copy-done.48), kind=kOutput, calls=%fused_computation.187 | convolution fusion | flops 939524096 | bytes 22052864 | tf_op jit(solution)/shard_map/dot_general | solution.py:132
  26.8 53.9 %collective-permute-done.2 = bf16[64,3,192]{0,2,1:T(8,128)(2,1)S(1)} collective-permute-done((bf16[64,3,192]{0,2,1:T(8,128)(2,1)}, bf16[64,3,192]{0,2,1:T(8,128)(2,1)S(1)}, u32[]{:S(2)}, u32[]{:S(2)}) %collective-permute-start.2) | collective-permute-done | bytes 73760 | tf_op jit(solution)/shard_map/ppermute | solution.py:18
  106.3 13.9 %fusion.3 = f32[64,832,128]{2,1,0:T(8,128)} fusion(bf16[64,192,128]{2,1,0:T(8,128)(2,1)} %collective-permute-done.1, bf16[64,448,128]{2,1,0:T(8,128)(2,1)} %param.11, bf16[64,192,128]{2,1,0:T(8,128)(2,1)} %collective-permute-done, bf16[256,128]{1,0:T(8,128)(2,1)S(1)} %copy-done.48), kind=kOutput, calls=%fused_computation.37 | convolution fusion | flops 1785724928 | bytes 40927232 | tf_op jit(solution)/shard_map/dot_general | solution.py:137
  120.1 28.5 %reshape_reshape.3 = f32[64,26,4096]{2,1,0:T(8,128)} reshape(f32[64,832,128]{2,1,0:T(8,128)} %fusion.3) | data formatting | bytes 54525952 | tf_op jit(solution)/shard_map/reshape;reshape | solution.py:35
  148.6 29.6 %subtract_convert_fusion = (bf16[64,26,4096]{2,1,0:T(8,128)(2,1)}, bf16[64,26,4096]{2,1,0:T(8,128)(2,1)S(1)}) fusion(f32[64,26,4096]{2,1,0:T(8,128)} %reshape_reshape.3), kind=kLoop, calls=%fused_computation.5 | loop fusion | flops 27262976 | bytes 54525952 | tf_op jit(solution)/shard_map/convert_element_type | solution.py:28
  178.2 7.1 fusion.52
  192.3 7.1 fusion.50
  199.4 7.4 fusion.49
  206.8 7.2 fusion.48
  221.0 7.1 fusion.46
  228.2 7.1 fusion.45
  235.3 18.9 %convolution_add_fusion.3 = f32[64,14,4096]{2,1,0:T(8,128)} fusion(f32[64,14,4096]{2,1,0:T(8,128)} %fusion.52, bf16[64,26,4096]{2,1,0:T(8,128)(2,1)} %get-tuple-element.18, s32[64,14]{1,0:T(8,128)S(1)} %copy.208), kind=kOutput, calls=%fused_computation.46 | convolution fusion | flops 194580736 | bytes 42995200 | tf_op jit(solution)/shard_map/fbc,fcx->fbx/dot_general | solution.py:46
  254.2 17.9 %reshape.371 = f32[64,14,32,128]{3,2,1,0:T(8,128)} reshape(f32[64,14,4096]{2,1,0:T(8,128)} %convolution_add_fusion.3) | data formatting | bytes 29360128 | tf_op jit(solution)/shard_map/reshape | solution.py:47
  272.1 18.9 %convolution_add_fusion.4 = f32[64,14,4096]{2,1,0:T(8,128)} fusion(f32[64,14,4096]{2,1,0:T(8,128)} %fusion.51, bf16[64,26,4096]{2,1,0:T(8,128)(2,1)} %get-tuple-element.18, s32[64,14]{1,0:T(8,128)S(1)} %copy.203), kind=kOutput, calls=%fused_computation.47 | convolution fusion | flops 194580736 | bytes 42995200 | tf_op jit(solution)/shard_map/fbc,fcx->fbx/dot_general | solution.py:46
  290.9 17.5 %reshape.370 = f32[64,14,32,128]{3,2,1,0:T(8,128)} reshape(f32[64,14,4096]{2,1,0:T(8,128)} %convolution_add_fusion.4) | data formatting | bytes 29360128 | tf_op jit(solution)/shard_map/reshape | solution.py:47
  308.4 18.9 %convolution_add_fusion.5 = f32[64,14,4096]{2,1,0:T(8,128)} fusion(f32[64,14,4096]{2,1,0:T(8,128)} %fusion.50, bf16[64,26,4096]{2,1,0:T(8,128)(2,1)} %get-tuple-element.18, s32[64,14]{1,0:T(8,128)S(1)} %copy.198), kind=kOutput, calls=%fused_computation.48 | convolution fusion | flops 194580736 | bytes 42995200 | tf_op jit(solution)/shard_map/fbc,fcx->fbx/dot_general | solution.py:46
  327.3 17.5 %reshape.369 = f32[64,14,32,128]{3,2,1,0:T(8,128)} reshape(f32[64,14,4096]{2,1,0:T(8,128)} %convolution_add_fusion.5) | data formatting | bytes 29360128 | tf_op jit(solution)/shard_map/reshape | solution.py:47
  344.8 19.0 %convolution_add_fusion.6 = f32[64,14,4096]{2,1,0:T(8,128)} fusion(f32[64,14,4096]{2,1,0:T(8,128)} %fusion.49, bf16[64,26,4096]{2,1,0:T(8,128)(2,1)} %get-tuple-element.18, s32[64,14]{1,0:T(8,128)S(1)} %copy-done.40), kind=kOutput, calls=%fused_computation.49 | convolution fusion | flops 194580736 | bytes 42995200 | tf_op jit(solution)/shard_map/fbc,fcx->fbx/dot_general | solution.py:46
  363.8 17.6 %reshape.368 = f32[64,14,32,128]{3,2,1,0:T(8,128)} reshape(f32[64,14,4096]{2,1,0:T(8,128)} %convolution_add_fusion.6) | data formatting | bytes 29360128 | tf_op jit(solution)/shard_map/reshape | solution.py:47
  381.4 19.0 %convolution_add_fusion.7 = f32[64,14,4096]{2,1,0:T(8,128)} fusion(f32[64,14,4096]{2,1,0:T(8,128)} %fusion.48, bf16[64,26,4096]{2,1,0:T(8,128)(2,1)} %get-tuple-element.18, s32[64,14]{1,0:T(8,128)S(1)} %copy-done.38), kind=kOutput, calls=%fused_computation.50 | convolution fusion | flops 194580736 | bytes 42995200 | tf_op jit(solution)/shard_map/fbc,fcx->fbx/dot_general | solution.py:46
  400.4 17.5 %reshape.367 = f32[64,14,32,128]{3,2,1,0:T(8,128)} reshape(f32[64,14,4096]{2,1,0:T(8,128)} %convolution_add_fusion.7) | data formatting | bytes 29360128 | tf_op jit(solution)/shard_map/reshape | solution.py:47
  417.9 18.9 %convolution_add_fusion.8 = f32[64,14,4096]{2,1,0:T(8,128)} fusion(f32[64,14,4096]{2,1,0:T(8,128)} %fusion.47, bf16[64,26,4096]{2,1,0:T(8,128)(2,1)} %get-tuple-element.18, s32[64,14]{1,0:T(8,128)S(1)} %copy-done.36), kind=kOutput, calls=%fused_computation.51 | convolution fusion | flops 194580736 | bytes 42995200 | tf_op jit(solution)/shard_map/fbc,fcx->fbx/dot_general | solution.py:46
  436.7 17.5 %reshape.366 = f32[64,14,32,128]{3,2,1,0:T(8,128)} reshape(f32[64,14,4096]{2,1,0:T(8,128)} %convolution_add_fusion.8) | data formatting | bytes 29360128 | tf_op jit(solution)/shard_map/reshape | solution.py:47
  454.2 18.9 %convolution_add_fusion.9 = f32[64,14,4096]{2,1,0:T(8,128)} fusion(f32[64,14,4096]{2,1,0:T(8,128)} %fusion.46, bf16[64,26,4096]{2,1,0:T(8,128)(2,1)} %get-tuple-element.18, s32[64,14]{1,0:T(8,128)S(1)} %copy-done.34), kind=kOutput, calls=%fused_computation.52 | convolution fusion | flops 194580736 | bytes 42995200 | tf_op jit(solution)/shard_map/fbc,fcx->fbx/dot_general | solution.py:46
  473.1 17.7 %reshape.365 = f32[64,14,32,128]{3,2,1,0:T(8,128)} reshape(f32[64,14,4096]{2,1,0:T(8,128)} %convolution_add_fusion.9) | data formatting | bytes 29360128 | tf_op jit(solution)/shard_map/reshape | solution.py:47
  490.8 18.9 %convolution_add_fusion.10 = f32[64,14,4096]{2,1,0:T(8,128)} fusion(f32[64,14,4096]{2,1,0:T(8,128)} %fusion.45, bf16[64,26,4096]{2,1,0:T(8,128)(2,1)} %get-tuple-element.18, s32[64,14]{1,0:T(8,128)S(1)} %copy-done.32), kind=kOutput, calls=%fused_computation.53 | convolution fusion | flops 194580736 | bytes 42995200 | tf_op jit(solution)/shard_map/fbc,fcx->fbx/dot_general | solution.py:46
  509.7 17.6 %reshape.364 = f32[64,14,32,128]{3,2,1,0:T(8,128)} reshape(f32[64,14,4096]{2,1,0:T(8,128)} %convolution_add_fusion.10) | data formatting | bytes 29360128 | tf_op jit(solution)/shard_map/reshape | solution.py:47
  527.5 20.7 %divide_multiply_fusion = f32[64,14,32,128]{3,2,1,0:T(8,128)} fusion(f32[128]{0:T(128)S(1)} %copy-done.53, f32[64,14,32,128]{3,2,1,0:T(8,128)} %bitcast.227, f32[64,14,32,128]{3,2,1,0:T(8,128)} %reshape.371, f32[64,14,32]{2,1,0:T(8,128)S(1)} %copy-done.16, f32[128]{0:T(128)S(1)} %copy-done.54, f32[128]{0:T(128)S(1)} %copy-done.52, ...), kind=kOutput, calls=%fused_computation.21 | convolution fusion | flops 990904320 | bytes 44189184 | tf_op jit(solution)/shard_map/dot_general | solution.py:56
  548.2 16.6 %divide_multiply_fusion.1 = f32[64,14,32,128]{3,2,1,0:T(8,128)} fusion(f32[128]{0:T(128)S(1)} %copy-done.53, f32[64,14,32,128]{3,2,1,0:T(8,128)S(1)} %bitcast.231, f32[64,14,32,128]{3,2,1,0:T(8,128)} %reshape.370, f32[64,14,32]{2,1,0:T(8,128)S(1)} %copy-done.18, f32[128]{0:T(128)S(1)} %copy-done.54, f32[128]{0:T(128)S(1)} %copy-done.52, ...), kind=kOutput, calls=%fused_computation.23 | convolution fusion | flops 990904320 | bytes 44189184 | tf_op jit(solution)/shard_map/dot_general | solution.py:56
  564.9 10.9 %divide_multiply_fusion.2 = f32[64,14,32,128]{3,2,1,0:T(8,128)} fusion(f32[128]{0:T(128)S(1)} %copy-done.53, f32[64,14,32,128]{3,2,1,0:T(8,128)S(1)} %bitcast.232, f32[64,14,32,128]{3,2,1,0:T(8,128)S(1)} %bitcast.243, f32[64,14,32]{2,1,0:T(8,128)S(1)} %copy-done.20, f32[128]{0:T(128)S(1)} %copy-done.54, f32[128]{0:T(128)S(1)} %copy-done.52, ...), kind=kOutput, calls=%fused_computation.25 | convolution fusion | flops 990904320 | bytes 44189184 | tf_op jit(solution)/shard_map/dot_general | solution.py:56
  575.8 17.8 %divide_multiply_fusion.3 = f32[64,14,32,128]{3,2,1,0:T(8,128)} fusion(f32[128]{0:T(128)S(1)} %copy-done.53, f32[64,14,32,128]{3,2,1,0:T(8,128)S(1)} %bitcast.233, f32[64,14,32,128]{3,2,1,0:T(8,128)} %reshape.368, f32[64,14,32]{2,1,0:T(8,128)S(1)} %copy-done.22, f32[128]{0:T(128)S(1)} %copy-done.54, f32[128]{0:T(128)S(1)} %copy-done.52, ...), kind=kOutput, calls=%fused_computation.27 | convolution fusion | flops 990904320 | bytes 44189184 | tf_op jit(solution)/shard_map/dot_general | solution.py:56
  593.6 10.9 %divide_multiply_fusion.4 = f32[64,14,32,128]{3,2,1,0:T(8,128)} fusion(f32[128]{0:T(128)S(1)} %copy-done.53, f32[64,14,32,128]{3,2,1,0:T(8,128)S(1)} %bitcast.234, f32[64,14,32,128]{3,2,1,0:T(8,128)S(1)} %copy-done.4, f32[64,14,32]{2,1,0:T(8,128)S(1)} %copy-done.24, f32[128]{0:T(128)S(1)} %copy-done.54, f32[128]{0:T(128)S(1)} %copy-done.52, ...), kind=kOutput, calls=%fused_computation.29 | convolution fusion | flops 990904320 | bytes 44189184 | tf_op jit(solution)/shard_map/dot_general | solution.py:56
  604.5 17.8 %divide_multiply_fusion.5 = f32[64,14,32,128]{3,2,1,0:T(8,128)} fusion(f32[128]{0:T(128)S(1)} %copy-done.53, f32[64,14,32,128]{3,2,1,0:T(8,128)S(1)} %bitcast.235, f32[64,14,32,128]{3,2,1,0:T(8,128)} %reshape.366, f32[64,14,32]{2,1,0:T(8,128)S(1)} %copy-done.26, f32[128]{0:T(128)S(1)} %copy-done.54, f32[128]{0:T(128)S(1)} %copy-done.52, ...), kind=kOutput, calls=%fused_computation.31 | convolution fusion | flops 990904320 | bytes 44189184 | tf_op jit(solution)/shard_map/dot_general | solution.py:56
  622.4 10.9 %divide_multiply_fusion.6 = f32[64,14,32,128]{3,2,1,0:T(8,128)} fusion(f32[128]{0:T(128)S(1)} %copy-done.53, f32[64,14,32,128]{3,2,1,0:T(8,128)S(1)} %bitcast.236, f32[64,14,32,128]{3,2,1,0:T(8,128)S(1)} %copy-done.5, f32[64,14,32]{2,1,0:T(8,128)S(1)} %copy-done.28, f32[128]{0:T(128)S(1)} %copy-done.54, f32[128]{0:T(128)S(1)} %copy-done.52, ...), kind=kOutput, calls=%fused_computation.33 | convolution fusion | flops 990904320 | bytes 44189184 | tf_op jit(solution)/shard_map/dot_general | solution.py:56
  633.2 52.7 %multiply_reduce_fusion.7 = (f32[64,14,32]{2,1,0:T(8,128)}, f32[64,14,32]{2,1,0:T(8,128)}, f32[64,14,32]{2,1,0:T(8,128)}, f32[64,14,32]{2,1,0:T(8,128)}, f32[64,...) fusion(f32[128]{0:T(128)S(1)} %copy-done.56, ...), kind=kOutput, calls=%fused_computation.17 | convolution fusion | flops 1082425344 | bytes 140527616 | tf_op jit(solution)/shard_map/dot_general | solution.py:56
  685.9 10.8 %copy.213 = bf16[64,448,128]{2,0,1:T(8,128)(2,1)} copy(bf16[64,448,128]{2,1,0:T(8,128)(2,1)} %bitcast.245) | data formatting | bytes 14680064 | tf_op jit(solution)/shard_map/reshape | solution.py:143
  703.8 47.5 %all-to-all-done = bf16[64,448,128]{2,0,1:T(8,128)(2,1)} async-done(((bf16[64,448,128]{2,0,1:T(8,128)(2,1)}), bf16[64,448,128]{2,0,1:T(8,128)(2,1)}, u32[]{:S(2)}, u32[]{:S(2)}) %all-to-all-start) | async-done | bytes 7340064 | tf_op jit(solution)/shard_map/all_to_all | solution.py:145
  751.3 7.8 copy.215
  762.2 8.1 fusion.11
  770.3 13.5 %fusion = bf16[128,28672]{1,0:T(8,128)(2,1)} fusion(f32[128,28672]{1,0:T(8,128)} %fusion.11, bf16[16,8,224,128]{3,2,1,0:T(8,128)(2,1)} %bitcast.226, f32[64,128]{1,0:T(8,128)S(1)} %get-tuple-element.66, f32[64,128]{1,0:T(8,128)S(1)} %get-tuple-element.67), kind=kOutput, calls=%fused_computation.3 | convolution fusion | flops 946946048 | bytes 29425664 | tf_op jit(solution)/shard_map/dot_general | solution.py:78
  811.6 14.5 %fusion.15 = f32[128,28672]{1,0:T(8,128)} fusion(f32[16,8,224,128]{3,2,1,0:T(8,128)S(1)} %bitcast.222, f32[128,64]{0,1:T(8,128)S(1)} %get-tuple-element.41, f32[128,64]{0,1:T(8,128)S(1)} %get-tuple-element.40), kind=kOutput, calls=%fused_computation.56 | convolution fusion | flops 939589632 | bytes 29425664 | tf_op jit(solution)/shard_map/dot_general | solution.py:100
  826.1 24.5 %convolution_add_fusion.1 = f32[128,28672]{1,0:T(8,128)} fusion(f32[128,28672]{1,0:T(8,128)} %fusion.15, f32[16,8,224,128]{3,2,1,0:T(8,128)} %bitcast.223, f32[128,64]{0,1:T(8,128)S(1)} %get-tuple-element.41, f32[128,64]{0,1:T(8,128)S(1)} %get-tuple-element.40), kind=kOutput, calls=%fused_computation.1 | convolution fusion | flops 943276032 | bytes 44105728 | tf_op jit(solution)/shard_map/dot_general | solution.py:101
  850.6 22.7 %fusion.16 = bf16[16,8,224,128]{3,1,2,0:T(8,128)(2,1)} fusion(f32[128,28672]{1,0:T(8,128)} %convolution_add_fusion.1, f32[16,8,224,128]{3,2,1,0:T(8,128)} %bitcast.224, f32[128,64]{0,1:T(8,128)S(1)} %get-tuple-element.41, f32[128,64]{0,1:T(8,128)S(1)} %get-tuple-element.40), kind=kOutput, calls=%fused_computation.57 | convolution fusion | flops 961609728 | bytes 36765696 | tf_op jit(solution)/shard_map/dot_general | solution.py:102
  873.3 7.8 copy.242
  888.0 12.7 %fusion.101 = f32[64,448,128]{2,1,0:T(8,128)} fusion(bf16[64,448,128]{2,1,0:T(8,128)(2,1)} %param.11, bf16[256,128]{1,0:T(8,128)(2,1)S(1)} %copy-done.49), kind=kOutput, calls=%fused_computation.189 | convolution fusion | flops 939524096 | bytes 22052864 | tf_op jit(solution)/shard_map/dot_general | solution.py:149
  911.4 25.3 %all-to-all-done.1 = bf16[128,224,128]{2,1,0:T(8,128)(2,1)} async-done(((bf16[128,224,128]{2,1,0:T(8,128)(2,1)}), bf16[128,224,128]{2,1,0:T(8,128)(2,1)}, u32[]{:S(2)}, u32[]{:S(2)}) %all-to-all-start.1) | async-done | bytes 7340064 | tf_op jit(solution)/shard_map/all_to_all | solution.py:147
  936.7 7.2 copy.216
  943.9 14.9 %add_convert_fusion = bf16[64,448,128]{2,1,0:T(8,128)(2,1)} fusion(bf16[64,448,128]{2,1,0:T(8,128)(2,1)} %param.11, f32[128]{0:T(128)S(1)} %get-tuple-element.39, f32[64,448,128]{2,1,0:T(8,128)} %fusion.101, bf16[64,448,128]{2,1,0:T(8,128)(2,1)} %bitcast.246, f32[128]{0:T(128)S(1)} %get-tuple-element.38, bf16[128,128]{1,0:T(8,128)(2,1)S(1)} %copy-done.55, ...), kind=kOutput, calls=%fused_computation.18 | convolution fusion | flops 1919418368 | bytes 36766720 | tf_op jit(solution)/shard_map/dot_general | solution.py:156
  (189 shorter events, 110.7 us)
Async XLA Ops:
  0.6 526.7 %copy-start = (bf16[128,128]{1,0:T(8,128)(2,1)S(1)}, bf16[128,128]{1,0:T(8,128)(2,1)}, u32[]{:S(2)}) copy-start(bf16[128,128]{1,0:T(8,128)(2,1)} %param.15) | copy-start | bytes 98308
  6.7 99.5 %collective-permute-start = (bf16[64,192,128]{2,1,0:T(8,128)(2,1)}, bf16[64,192,128]{2,1,0:T(8,128)(2,1)}, u32[]{:S(2)}, u32[]{:S(2)}) collective-permute-start(bf16[64,192,128]{2,1,0:T(8,128)(2,1)} %get-tuple-element.23), channel_id=1, source_target_pairs={{0,2},{2,4},{4,6},{6,8},{8,10},{10,12},{12,14},{14,16},{16,18},{18... | collective-permute-start | bytes 9437192 | tf_op jit(solution)/shard_map/ppermute | solution.py:18
  9.3 96.9 %collective-permute-start.1 = (bf16[64,192,128]{2,1,0:T(8,128)(2,1)}, bf16[64,192,128]{2,1,0:T(8,128)(2,1)}, u32[]{:S(2)}, u32[]{:S(2)}) collective-permute-start(bf16[64,192,128]{2,1,0:T(8,128)(2,1)} %get-tuple-element.24), channel_id=1, source_target_pairs={{2,0},{4,2},{6,4},{8,6},{10,8},{12,10},{14,12},{16,14},{18,16},{20... | collective-permute-start | bytes 9437192 | tf_op jit(solution)/shard_map/ppermute | solution.py:21
  11.4 69.3 %collective-permute-start.2 = (bf16[64,3,192]{0,2,1:T(8,128)(2,1)}, bf16[64,3,192]{0,2,1:T(8,128)(2,1)S(1)}, u32[]{:S(2)}, u32[]{:S(2)}) collective-permute-start(bf16[64,3,192]{0,2,1:T(8,128)(2,1)} %get-tuple-element.25), channel_id=1, source_target_pairs={{0,2},{2,4},{4,6},{6,8},{8,10},{10,12},{12,14},{14,16},{16,18},{18... | collective-permute-start | bytes 221192 | tf_op jit(solution)/shard_map/ppermute | solution.py:18
  13.2 69.9 %collective-permute-start.3 = (bf16[64,3,192]{0,2,1:T(8,128)(2,1)S(1)}, bf16[64,3,192]{0,2,1:T(8,128)(2,1)S(1)}, u32[]{:S(2)}, u32[]{:S(2)}) collective-permute-start(bf16[64,3,192]{0,2,1:T(8,128)(2,1)S(1)} %get-tuple-element.26), channel_id=1, source_target_pairs={{2,0},{4,2},{6,4},{8,6},{10,8},{12,10},{14,12},{16,14},{18,16},{20... | collective-permute-start | bytes 221192 | tf_op jit(solution)/shard_map/ppermute | solution.py:21
  26.4 173.0 %copy-start.39 = (s32[64,14]{1,0:T(8,128)}, s32[64,14]{1,0:T(8,128)S(1)}, u32[]{:S(2)}) copy-start(s32[64,14]{1,0:T(8,128)S(1)} %copy.193) | copy-start | bytes 10756
  26.5 180.3 %copy-start.37 = (s32[64,14]{1,0:T(8,128)}, s32[64,14]{1,0:T(8,128)S(1)}, u32[]{:S(2)}) copy-start(s32[64,14]{1,0:T(8,128)S(1)} %copy.188) | copy-start | bytes 10756
  26.6 187.4 %copy-start.35 = (s32[64,14]{1,0:T(8,128)}, s32[64,14]{1,0:T(8,128)S(1)}, u32[]{:S(2)}) copy-start(s32[64,14]{1,0:T(8,128)S(1)} %copy.183) | copy-start | bytes 10756
  26.7 194.3 %copy-start.33 = (s32[64,14]{1,0:T(8,128)}, s32[64,14]{1,0:T(8,128)S(1)}, u32[]{:S(2)}) copy-start(s32[64,14]{1,0:T(8,128)S(1)} %copy.178) | copy-start | bytes 10756
  26.8 201.3 %copy-start.31 = (s32[64,14]{1,0:T(8,128)}, s32[64,14]{1,0:T(8,128)S(1)}, u32[]{:S(2)}) copy-start(s32[64,14]{1,0:T(8,128)S(1)} %copy.171) | copy-start | bytes 10756
  327.3 17.5 %copy-start.40 = (s32[64,14]{1,0:T(8,128)S(1)}, s32[64,14]{1,0:T(8,128)}, u32[]{:S(2)}) copy-start(s32[64,14]{1,0:T(8,128)} %copy-done.39) | copy-start | bytes 10756
  363.8 17.6 %copy-start.38 = (s32[64,14]{1,0:T(8,128)S(1)}, s32[64,14]{1,0:T(8,128)}, u32[]{:S(2)}) copy-start(s32[64,14]{1,0:T(8,128)} %copy-done.37) | copy-start | bytes 10756
  400.4 17.5 %copy-start.36 = (s32[64,14]{1,0:T(8,128)S(1)}, s32[64,14]{1,0:T(8,128)}, u32[]{:S(2)}) copy-start(s32[64,14]{1,0:T(8,128)} %copy-done.35) | copy-start | bytes 10756
  436.7 17.5 %copy-start.34 = (s32[64,14]{1,0:T(8,128)S(1)}, s32[64,14]{1,0:T(8,128)}, u32[]{:S(2)}) copy-start(s32[64,14]{1,0:T(8,128)} %copy-done.33) | copy-start | bytes 10756
  473.1 17.7 %copy-start.32 = (s32[64,14]{1,0:T(8,128)S(1)}, s32[64,14]{1,0:T(8,128)}, u32[]{:S(2)}) copy-start(s32[64,14]{1,0:T(8,128)} %copy-done.31) | copy-start | bytes 10756
  509.7 17.7 %copy-start.16 = (f32[64,14,32]{2,1,0:T(8,128)S(1)}, f32[64,14,32]{2,1,0:T(8,128)}, u32[]{:S(2)}) copy-start(f32[64,14,32]{2,1,0:T(8,128)} %get-tuple-element.56) | copy-start | bytes 344068
  509.7 17.7 %copy-start.52 = (f32[128]{0:T(128)S(1)}, f32[128]{0:T(128)}, u32[]{:S(2)}) copy-start(f32[128]{0:T(128)} %get-tuple-element.35) | copy-start | bytes 1540
  509.7 17.7 %copy-start.53 = (f32[128]{0:T(128)S(1)}, f32[128]{0:T(128)}, u32[]{:S(2)}) copy-start(f32[128]{0:T(128)} %get-tuple-element.36) | copy-start | bytes 1540
  509.7 17.7 %copy-start.54 = (f32[128]{0:T(128)S(1)}, f32[128]{0:T(128)}, u32[]{:S(2)}) copy-start(f32[128]{0:T(128)} %get-tuple-element.37) | copy-start | bytes 1540
  509.7 38.4 %slice-start = ((s8[14680064]{0:T(1024)(128)(4,1)}), s8[2097152]{0:T(1024)(128)(4,1)S(1)}, s32[]{:S(2)}) async-start(s8[14680064]{0:T(1024)(128)(4,1)} %bitcast.229), calls=%async_computation.2 | async-start | bytes 4194304
  527.4 20.8 %slice-start.1 = ((s8[14680064]{0:T(1024)(128)(4,1)}), s8[4194304]{0:T(1024)(128)(4,1)S(1)}, s32[]{:S(2)}) async-start(s8[14680064]{0:T(1024)(128)(4,1)} %bitcast.229), calls=%async_computation.3 | async-start | bytes 8388608
  527.4 20.8 %slice-start.2 = ((s8[14680064]{0:T(1024)(128)(4,1)}), s8[4194304]{0:T(1024)(128)(4,1)S(1)}, s32[]{:S(2)}) async-start(s8[14680064]{0:T(1024)(128)(4,1)} %bitcast.229), calls=%async_computation.4 | async-start | bytes 8388608
  527.4 20.8 %slice-start.3 = ((s8[14680064]{0:T(1024)(128)(4,1)}), s8[4194304]{0:T(1024)(128)(4,1)S(1)}, s32[]{:S(2)}) async-start(s8[14680064]{0:T(1024)(128)(4,1)} %bitcast.229), calls=%async_computation.5 | async-start | bytes 8388608
  527.4 20.8 %copy-start.18 = (f32[64,14,32]{2,1,0:T(8,128)S(1)}, f32[64,14,32]{2,1,0:T(8,128)}, u32[]{:S(2)}) copy-start(f32[64,14,32]{2,1,0:T(8,128)} %get-tuple-element.54) | copy-start | bytes 344068
  527.4 37.4 %slice-start.4 = ((s8[14680064]{0:T(1024)(128)(4,1)}), s8[4194304]{0:T(1024)(128)(4,1)S(1)}, s32[]{:S(2)}) async-start(s8[14680064]{0:T(1024)(128)(4,1)} %bitcast.242), calls=%async_computation.6 | async-start | bytes 8388608
  527.4 37.4 %slice-start.5 = ((s8[14680064]{0:T(1024)(128)(4,1)}), s8[4194304]{0:T(1024)(128)(4,1)S(1)}, s32[]{:S(2)}) async-start(s8[14680064]{0:T(1024)(128)(4,1)} %bitcast.242), calls=%async_computation.7 | async-start | bytes 8388608
  548.2 16.7 %slice-start.6 = ((s8[14680064]{0:T(1024)(128)(4,1)}), s8[4194304]{0:T(1024)(128)(4,1)S(1)}, s32[]{:S(2)}) async-start(s8[14680064]{0:T(1024)(128)(4,1)} %bitcast.242), calls=%async_computation.8 | async-start | bytes 8388608
  548.2 16.6 %slice-start.7 = ((s8[14680064]{0:T(1024)(128)(4,1)}), s8[2097152]{0:T(1024)(128)(4,1)S(1)}, s32[]{:S(2)}) async-start(s8[14680064]{0:T(1024)(128)(4,1)} %bitcast.242), calls=%async_computation.9 | async-start | bytes 4194304
  548.2 16.6 %copy-start.20 = (f32[64,14,32]{2,1,0:T(8,128)S(1)}, f32[64,14,32]{2,1,0:T(8,128)}, u32[]{:S(2)}) copy-start(f32[64,14,32]{2,1,0:T(8,128)} %get-tuple-element.52) | copy-start | bytes 344068
  575.8 17.9 %copy-start.4 = (f32[64,14,32,128]{3,2,1,0:T(8,128)S(1)}, f32[64,14,32,128]{3,2,1,0:T(8,128)}, u32[]{:S(2)}) copy-start(f32[64,14,32,128]{3,2,1,0:T(8,128)} %reshape.367) | copy-start | bytes 44040196
  575.8 17.9 %copy-start.24 = (f32[64,14,32]{2,1,0:T(8,128)S(1)}, f32[64,14,32]{2,1,0:T(8,128)}, u32[]{:S(2)}) copy-start(f32[64,14,32]{2,1,0:T(8,128)} %get-tuple-element.48) | copy-start | bytes 344068
  604.5 17.9 %copy-start.5 = (f32[64,14,32,128]{3,2,1,0:T(8,128)S(1)}, f32[64,14,32,128]{3,2,1,0:T(8,128)}, u32[]{:S(2)}) copy-start(f32[64,14,32,128]{3,2,1,0:T(8,128)} %reshape.365) | copy-start | bytes 44040196
  604.5 17.9 %copy-start.28 = (f32[64,14,32]{2,1,0:T(8,128)S(1)}, f32[64,14,32]{2,1,0:T(8,128)}, u32[]{:S(2)}) copy-start(f32[64,14,32]{2,1,0:T(8,128)} %get-tuple-element.44) | copy-start | bytes 344068
  696.8 54.5 %all-to-all-start = ((bf16[64,448,128]{2,0,1:T(8,128)(2,1)}), bf16[64,448,128]{2,0,1:T(8,128)(2,1)}, u32[]{:S(2)}, u32[]{:S(2)}) async-start(bf16[64,448,128]{2,0,1:T(8,128)(2,1)} %copy.213), calls=%async_computation | async-start | bytes 14680064 | tf_op jit(solution)/shard_map/all_to_all | solution.py:145
  881.1 55.6 %all-to-all-start.1 = ((bf16[128,224,128]{2,1,0:T(8,128)(2,1)}), bf16[128,224,128]{2,1,0:T(8,128)(2,1)}, u32[]{:S(2)}, u32[]{:S(2)}) async-start(bf16[128,224,128]{2,1,0:T(8,128)(2,1)} %bitcast.241), calls=%async_computation.1 | async-start | bytes 14680064 | tf_op jit(solution)/shard_map/all_to_all | solution.py:147
  887.8 15.5 %copy-start.21 = (f32[64,14,32]{2,1,0:T(8,128)S(1)}, f32[64,14,32]{2,1,0:T(8,128)}, u32[]{:S(2)}) copy-start(f32[64,14,32]{2,1,0:T(8,128)} %get-tuple-element.52) | copy-start | bytes 344068
  887.8 15.5 %copy-start.23 = (f32[64,14,32]{2,1,0:T(8,128)S(1)}, f32[64,14,32]{2,1,0:T(8,128)}, u32[]{:S(2)}) copy-start(f32[64,14,32]{2,1,0:T(8,128)} %get-tuple-element.50) | copy-start | bytes 344068
  887.9 16.8 %copy-start.17 = (f32[64,14,32]{2,1,0:T(8,128)S(1)}, f32[64,14,32]{2,1,0:T(8,128)}, u32[]{:S(2)}) copy-start(f32[64,14,32]{2,1,0:T(8,128)} %get-tuple-element.56) | copy-start | bytes 344068
  887.9 16.8 %copy-start.19 = (f32[64,14,32]{2,1,0:T(8,128)S(1)}, f32[64,14,32]{2,1,0:T(8,128)}, u32[]{:S(2)}) copy-start(f32[64,14,32]{2,1,0:T(8,128)} %get-tuple-element.54) | copy-start | bytes 344068
  887.9 18.2 %copy-start.8 = (f32[64,3,14,32]{3,2,1,0:T(8,128)S(1)}, f32[64,3,14,32]{3,2,1,0:T(8,128)}, u32[]{:S(2)}) copy-start(f32[64,3,14,32]{3,2,1,0:T(8,128)} %get-tuple-element.57) | copy-start | bytes 1032196
  887.9 18.2 %copy-start.9 = (f32[64,3,14,32]{3,2,1,0:T(8,128)S(1)}, f32[64,3,14,32]{3,2,1,0:T(8,128)}, u32[]{:S(2)}) copy-start(f32[64,3,14,32]{3,2,1,0:T(8,128)} %get-tuple-element.55) | copy-start | bytes 1032196
  887.9 18.1 %copy-start.10 = (f32[64,3,14,32]{3,2,1,0:T(8,128)S(1)}, f32[64,3,14,32]{3,2,1,0:T(8,128)}, u32[]{:S(2)}) copy-start(f32[64,3,14,32]{3,2,1,0:T(8,128)} %get-tuple-element.53) | copy-start | bytes 1032196
  887.9 18.1 %copy-start.11 = (f32[64,3,14,32]{3,2,1,0:T(8,128)S(1)}, f32[64,3,14,32]{3,2,1,0:T(8,128)}, u32[]{:S(2)}) copy-start(f32[64,3,14,32]{3,2,1,0:T(8,128)} %get-tuple-element.51) | copy-start | bytes 1032196
  887.9 18.1 %copy-start.12 = (f32[64,3,14,32]{3,2,1,0:T(8,128)S(1)}, f32[64,3,14,32]{3,2,1,0:T(8,128)}, u32[]{:S(2)}) copy-start(f32[64,3,14,32]{3,2,1,0:T(8,128)} %get-tuple-element.49) | copy-start | bytes 1032196
  887.9 18.1 %copy-start.13 = (f32[64,3,14,32]{3,2,1,0:T(8,128)S(1)}, f32[64,3,14,32]{3,2,1,0:T(8,128)}, u32[]{:S(2)}) copy-start(f32[64,3,14,32]{3,2,1,0:T(8,128)} %get-tuple-element.47) | copy-start | bytes 1032196
  887.9 18.1 %copy-start.14 = (f32[64,3,14,32]{3,2,1,0:T(8,128)S(1)}, f32[64,3,14,32]{3,2,1,0:T(8,128)}, u32[]{:S(2)}) copy-start(f32[64,3,14,32]{3,2,1,0:T(8,128)} %get-tuple-element.45) | copy-start | bytes 1032196
  888.0 18.1 %copy-start.15 = (f32[64,3,14,32]{3,2,1,0:T(8,128)S(1)}, f32[64,3,14,32]{3,2,1,0:T(8,128)}, u32[]{:S(2)}) copy-start(f32[64,3,14,32]{3,2,1,0:T(8,128)} %get-tuple-element.43) | copy-start | bytes 1032196
  906.1 37.7 %copy-start.55 = (bf16[128,128]{1,0:T(8,128)(2,1)S(1)}, bf16[128,128]{1,0:T(8,128)(2,1)}, u32[]{:S(2)}) copy-start(bf16[128,128]{1,0:T(8,128)(2,1)} %param.20) | copy-start | bytes 98308
  (23 other events, 269.1 us)
where the time goes:
time: 967 us; the launch traced here: 959 us
  matrix products  533 us (55%)
  local copies, waits for them, and re-layouts  231 us (24%)
  waiting for transfers between devices  129 us (13%)
  other arithmetic  46.4 us (5%)
  starting transfers between devices  18.9 us (2%)
    dot_general x8, matrix products, edge_pass(): jnp.dot(hidden.reshape(-1, feat_width), edge_out, preferred_element_type=...  158 us
    dot_general x8, matrix products, edge_pass(): jnp.einsum('fbc,fcx->fbx', select_bf, dst_low, preferred_element_type=jnp...  151 us
    reshape x8, local copies, waits for them, and re-layouts, edge_pass(): near_dst = near_dst.reshape(own_src.shape)  141 us
    dot_general x8, matrix products, edge_pass(): jnp.einsum('fbc,fcx->fbx', select_bf, dst_high, preferred_element_type=jn...  57.1 us
    ppermute x2, waiting for transfers between devices, with_halo(): lax.ppermute(lax.slice_in_dim(block, block.shape[dim] - width, None, axis...  53.9 us
    all_to_all x1, waiting for transfers between devices, shards(): lax.all_to_all(mean_msg, 'tm', split_axis=1, concat_axis=0, tiled=True)  47.5 us
    convert_element_type x1, other arithmetic, split_parts(): low_part = (values - high_part.astype(jnp.float32)).astype(jnp.bfloat16)  29.6 us
    another operation x1, local copies, waits for them, and re-layouts, edge_pass(): flat_dst = other_dst.reshape(frames, other_blocks, block_len * feat_width)  28.5 us
  transfers between devices with their start and end apart: 6, of which 4 were waited for; matrix products, arithmetic and copies ran while one was open for 6% of the time, Pallas kernels for 0%

commit v1 on v0

v1 whole, which is shorter than its diff:
```python
import functools
import math

import jax
import jax.numpy as jnp
from jax import lax
from jax.experimental import pallas as pl
from jax.experimental.pallas import tpu as pltpu
from jax.sharding import PartitionSpec as P

BLOCK = 32
GHOST = 6
STEP = 8


def silu_half(half):
    return half + half * jnp.tanh(half)


def edge_body(picked, rank, *refs, table, base, first, count, parts, start):
    if table == "own":
        feats, rows, edge_in, edge_out, params, coord = refs[:6]
        rest = refs[6:]
    else:
        feats, rows, halo, edge_in, edge_out, params, coord = refs[:7]
        rest = refs[7:]
    outs, moved = rest[:parts], rest[parts]
    dst, src, near, spots, sums, hid = rest[parts + 1 :]
    width = edge_out.shape[1]
    slots = picked.shape[1] // (feats.shape[1] // BLOCK)
    ghost_rows = GHOST * BLOCK
    step = pl.program_id(0)
    w_src = edge_in[:width] * 0.5
    w_dst = edge_in[width:] * 0.5
    w_out = edge_out[...] * 0.5
    bias_in = params[0:1] * 0.5
    slope = params[1:2] * 0.5
    bias_out = params[2:3] * 0.5
    coord_high = coord[...].astype(jnp.bfloat16)
    coord_low = (coord[...] - coord_high.astype(jnp.float32)).astype(jnp.bfloat16)
    coord_rows = jnp.concatenate(
        [jnp.broadcast_to(coord_high, (slots, width)), jnp.broadcast_to(coord_low, (slots, width))],
        axis=0,
    )
    lane = lax.broadcasted_iota(jnp.int32, (slots, width), 1) // BLOCK
    sub = lax.broadcasted_iota(jnp.int32, (slots, width), 0)
    per = width // BLOCK
    masks = [lane + per * q == sub for q in range(slots // per)]

    def frame(f, carry):
        own_rows = feats.shape[1]
        if table == "low":
            dst[:ghost_rows] = jnp.dot(
                halo[f, :ghost_rows], w_dst, preferred_element_type=jnp.float32
            )
            keep = (first + count + GHOST) * BLOCK
            dst[ghost_rows : ghost_rows + keep] = jnp.dot(
                feats[f, :keep], w_dst, preferred_element_type=jnp.float32
            )
            spots[:8] = halo[f, ghost_rows:].astype(jnp.float32)
            spots[8:24] = rows[f]
            row_of, own_at = 2, 8
        elif table == "high":
            skip = (first - GHOST) * BLOCK
            dst[skip:own_rows] = jnp.dot(
                feats[f, skip:], w_dst, preferred_element_type=jnp.float32
            )
            dst[own_rows : own_rows + ghost_rows] = jnp.dot(
                halo[f, :ghost_rows], w_dst, preferred_element_type=jnp.float32
            )
            spots[:16] = rows[f]
            blocks = own_rows // BLOCK
            spots[blocks : blocks + 8] = halo[f, ghost_rows:].astype(jnp.float32)
            row_of, own_at = 0, 0
        else:
            dst[:own_rows] = jnp.dot(feats[f], w_dst, preferred_element_type=jnp.float32)
            spots[:16] = rows[f]
            row_of, own_at = 0, 0
        src[...] = (
            jnp.dot(
                feats[f, first * BLOCK : (first + count) * BLOCK],
                w_src,
                preferred_element_type=jnp.float32,
            )
            + bias_in
        )
        at = start + step * STEP + f
        for b in range(count):
            chosen = [picked[at, (first + b) * slots + s] - base for s in range(slots)]
            for s in range(slots):
                near[b * slots + s : b * slots + s + 1] = spots[pl.ds(chosen[s] + row_of, 1)]
            here = spots[own_at + first + b : own_at + first + b + 1]
            offset = here - near[b * slots : (b + 1) * slots]
            square = offset * offset
            dist = square + pltpu.roll(square, width // 2, 1)
            dist = dist + pltpu.roll(dist, width // 4, 1)
            gain = offset / (1.0 + jnp.sqrt(dist + 1.0))
            dist_t = jnp.transpose(dist)[:BLOCK]
            own = src[b * BLOCK : (b + 1) * BLOCK]
            for s in range(slots):
                other = dst[pl.ds(pl.multiple_of(chosen[s] * BLOCK, BLOCK), BLOCK)]
                pre = own + other + dist_t[:, s : s + 1] * slope
                hid[b % 2, s * BLOCK : (s + 1) * BLOCK] = silu_half(pre).astype(jnp.bfloat16)
            act = jnp.dot(hid[b % 2], w_out, preferred_element_type=jnp.float32) + bias_out
            message = silu_half(act)
            total = message[:BLOCK]
            for s in range(1, slots):
                total = total + message[s * BLOCK : (s + 1) * BLOCK]
            sums[pl.ds(b * BLOCK * STEP + f, BLOCK, stride=STEP), :] = total
            weight = lax.dot_general(
                coord_rows,
                message.astype(jnp.bfloat16),
                (((1,), (1,)), ((), ())),
                preferred_element_type=jnp.float32,
            )
            weight = weight[:slots] + weight[slots:]
            spread = jnp.zeros((slots, width), jnp.float32)
            for q, mask in enumerate(masks):
                spread = jnp.where(mask, weight[:, q * width : (q + 1) * width], spread)
            spread = spread + pltpu.roll(spread, width // 2, 1)
            spread = spread + pltpu.roll(spread, width // 4, 1)
            moved[f, b : b + 1] = jnp.sum(gain * spread, axis=0, keepdims=True) * (1.0 / slots)
        return carry

    lax.fori_loop(0, STEP, frame, 0)
    share = count * BLOCK // parts
    for r in range(parts):
        part = lax.rem(rank[0] + r, parts)
        block = sums[pl.ds(pl.multiple_of(part * share * STEP, STEP), share * STEP)]
        outs[r][...] = (
            (block * (1.0 / slots)).astype(jnp.bfloat16).reshape(share, STEP, width)
        )


def edge_call(
    rank, picked, feats, rows, halo, weights, *, table, first, count, start, frames, parts
):
    width = feats.shape[2]
    own_rows = feats.shape[1]
    slots = picked.shape[1] // (own_rows // BLOCK)
    shift = start // STEP
    share = count * BLOCK // parts
    ins = [
        pl.BlockSpec((STEP, own_rows, width), lambda i, *_: (i + shift, 0, 0)),
        pl.BlockSpec((STEP,) + rows.shape[1:], lambda i, *_: (i + shift, 0, 0)),
    ]
    args = [feats, rows]
    if halo is not None:
        ins.append(pl.BlockSpec((STEP,) + halo.shape[1:], lambda i, *_: (i, 0, 0)))
        args.append(halo)
    for w in weights:
        ins.append(pl.BlockSpec(w.shape, lambda i, *_: (0, 0)))
    out_shape = [jax.ShapeDtypeStruct((share, frames, width), jnp.bfloat16)] * parts
    out_specs = [pl.BlockSpec((share, STEP, width), lambda i, *_: (0, i, 0))] * parts
    out_shape.append(jax.ShapeDtypeStruct((frames, count, width), jnp.float32))
    out_specs.append(pl.BlockSpec((STEP, count, width), lambda i, *_: (i, 0, 0)))
    edges = frames * count * BLOCK * slots
    base = 0 if table == "low" else GHOST
    return pl.pallas_call(
        functools.partial(
            edge_body, table=table, base=base, first=first, count=count, parts=parts, start=start
        ),
        out_shape=out_shape,
        grid_spec=pltpu.PrefetchScalarGridSpec(
            num_scalar_prefetch=2,
            grid=(frames // STEP,),
            in_specs=ins,
            out_specs=out_specs,
            scratch_shapes=[
                pltpu.VMEM((own_rows + GHOST * BLOCK, width), jnp.float32),
                pltpu.VMEM((count * BLOCK, width), jnp.float32),
                pltpu.VMEM((count * slots, width), jnp.float32),
                pltpu.VMEM((32, width), jnp.float32),
                pltpu.VMEM((count * BLOCK * STEP, width), jnp.float32),
                pltpu.VMEM((2, slots * BLOCK, width), jnp.bfloat16),
            ],
        ),
        cost_estimate=pl.CostEstimate(
            flops=edges * width * width * 16, bytes_accessed=edges * 16, transcendentals=0
        ),
        name=f"edge_{table}",
    )(picked, rank, *args, *weights)


def spectral_body(*refs, pieces, parts):
    data = refs[:pieces]
    fwd, inv, mixer = refs[pieces : pieces + 3]
    outs = refs[pieces + 3 : pieces + 3 + parts]
    coef, mixed = refs[pieces + 3 + parts :]
    items, _, width = data[0].shape
    modes = mixer.shape[1]
    total = 2 * modes
    times = inv.shape[1]
    fwd_high, fwd_low = fwd[0], fwd[1]
    inv_high, inv_low = inv[0], inv[1]

    def forward(n, carry):
        column = jnp.concatenate([d[n] for d in data], axis=0)
        value = jnp.dot(fwd_high, column, preferred_element_type=jnp.float32) + jnp.dot(
            fwd_low, column, preferred_element_type=jnp.float32
        )
        coef[pl.ds(n, total, stride=items), :] = value
        return carry

    lax.fori_loop(0, items, forward, 0, unroll=2)

    def mix(k, carry):
        real = coef[pl.ds(pl.multiple_of(k * items, 8), items)].astype(jnp.bfloat16)
        imag = coef[pl.ds(pl.multiple_of((k + modes) * items, 8), items)].astype(jnp.bfloat16)
        w_real, w_imag = mixer[0, k], mixer[1, k]
        left = jnp.concatenate([real, imag], axis=1)
        right = jnp.concatenate(
            [
                jnp.concatenate([w_real, w_imag], axis=1),
                jnp.concatenate([-w_imag, w_real], axis=1),
            ],
            axis=0,
        )
        value = jnp.dot(left, right, preferred_element_type=jnp.float32)
        mixed[pl.ds(k, items, stride=total), :] = value[:, :width]
        mixed[pl.ds(k + modes, items, stride=total), :] = value[:, width:]
        return carry

    lax.fori_loop(0, modes, mix, 0, unroll=2)

    def backward(n, carry):
        column = mixed[pl.ds(pl.multiple_of(n * total, 8), total)]
        high = column.astype(jnp.bfloat16)
        low = (column - high.astype(jnp.float32)).astype(jnp.bfloat16)
        value = (
            jnp.dot(inv_high, high, preferred_element_type=jnp.float32)
            + jnp.dot(inv_low, high, preferred_element_type=jnp.float32)
            + jnp.dot(inv_high, low, preferred_element_type=jnp.float32)
        )
        coef[pl.ds(n, times, stride=items), :] = value
        return carry

    lax.fori_loop(0, items, backward, 0, unroll=2)
    span = times // parts
    for r in range(parts):
        block = coef[r * span * items : (r + 1) * span * items].astype(jnp.bfloat16)
        outs[r][...] = block.reshape(span, items, width)


def spectral_call(data, fwd, inv, mixer, parts):
    items, _, width = data[0].shape
    times = inv.shape[1]
    total = 2 * mixer.shape[1]
    span = times // parts
    flops = items * width * (4 * total * times + 4 * total * width + 6 * total * times)
    return pl.pallas_call(
        functools.partial(spectral_body, pieces=len(data), parts=parts),
        out_shape=[jax.ShapeDtypeStruct((span, items, width), jnp.bfloat16)] * parts,
        scratch_shapes=[
            pltpu.VMEM((max(total, times) * items, width), jnp.float32),
            pltpu.VMEM((total * items, width), jnp.float32),
        ],
        cost_estimate=pl.CostEstimate(
            flops=flops * 4, bytes_accessed=items * times * width * 4, transcendentals=0
        ),
        name="spectral",
    )(*data, fwd, inv, mixer)


def node_body(spot, *refs):
    feats, conv, node_in, node_out, bias, out = refs[0], refs[1], refs[2], refs[3], refs[4], refs[-1]
    frames, rows, width = feats.shape
    w_in = node_in[...] * 0.5
    first_bias = bias[0:1] * 0.5
    group = max(1, min(frames, 256 // rows))

    def chunk(i, carry):
        pick = pl.ds(pl.multiple_of(i * group, group), group)
        x = feats[pick].reshape(group * rows, width)
        c = conv[pick].reshape(group * rows, width)
        pre = (
            jnp.dot(
                jnp.concatenate([x, c], axis=1), w_in, preferred_element_type=jnp.float32
            )
            + first_bias
        )
        hidden = silu_half(pre).astype(jnp.bfloat16)
        value = x.astype(jnp.float32) + (
            jnp.dot(hidden, node_out[...], preferred_element_type=jnp.float32) + bias[1:2]
        )
        out[pick] = value.astype(jnp.bfloat16).reshape(group, rows, width)
        return carry

    lax.fori_loop(0, frames // group, chunk, 0)


def node_call(spot, feats, conv, weights, buffer, rows):
    frames, particles, width = feats.shape
    items = conv.shape[1]
    ins = [
        pl.BlockSpec((frames, rows, width), lambda i, s: (0, s[0] + i, 0)),
        pl.BlockSpec((frames, rows, width), lambda i, s: (0, i, 0)),
    ]
    for w in weights:
        ins.append(pl.BlockSpec(w.shape, lambda i, s: (0, 0)))
    args = [feats, conv, *weights]
    aliases = {}
    if buffer is not None:
        ins.append(pl.BlockSpec(memory_space=pl.ANY))
        args.append(buffer)
        aliases = {len(args): 0}
    return pl.pallas_call(
        node_body,
        out_shape=jax.ShapeDtypeStruct(feats.shape, jnp.bfloat16),
        grid_spec=pltpu.PrefetchScalarGridSpec(
            num_scalar_prefetch=1,
            grid=(items // rows,),
            in_specs=ins,
            out_specs=pl.BlockSpec((frames, rows, width), lambda i, s: (0, s[0] + i, 0)),
        ),
        input_output_aliases=aliases,
        cost_estimate=pl.CostEstimate(
            flops=frames * items * width * width * 12,
            bytes_accessed=frames * items * width * 6,
            transcendentals=0,
        ),
        name="node",
    )(spot, *args)


def split_parts(values):
    high_part = values.astype(jnp.bfloat16)
    low_part = (values - high_part.astype(jnp.float32)).astype(jnp.bfloat16)
    return jnp.stack([high_part, low_part])


def transforms(rank, parts, frames, modes):
    times = parts * frames
    step_angle = 2.0 * math.pi / times
    local = jnp.arange(frames, dtype=jnp.int32)
    ranks = jnp.arange(parts, dtype=jnp.int32)
    mode_ids = jnp.arange(modes, dtype=jnp.int32)
    from_times = (((rank - ranks) % parts)[:, None] * frames + local).reshape(-1)
    to_times = (((rank + ranks) % parts)[:, None] * frames + local).reshape(-1)
    angles = (mode_ids[:, None] * from_times[None, :] % times).astype(jnp.float32) * step_angle
    forward = jnp.concatenate([jnp.cos(angles), -jnp.sin(angles)], axis=0)
    back = (to_times[:, None] * mode_ids[None, :] % times).astype(jnp.float32) * step_angle
    weights = (jnp.where(mode_ids == 0, 1.0, 2.0) / times).astype(jnp.float32)
    inverse = jnp.concatenate([jnp.cos(back) * weights, -jnp.sin(back) * weights], axis=1)
    return split_parts(forward), split_parts(inverse)


def cut(frames, fractions):
    if frames < 64:
        return [(0, frames)]
    sizes = [frames * a // 64 for a in fractions]
    return [(sum(sizes[:i]), size) for i, size in enumerate(sizes)]


def shards(
    node_feats,
    positions,
    neighbours,
    edge_in,
    edge_out,
    edge_params,
    coord_weight,
    spectral,
    node_in,
    node_out,
    node_bias,
):
    frames, local_rows, width = node_feats.shape
    blocks = local_rows // BLOCK
    rim = GHOST * BLOCK
    parts = lax.axis_size("tm")
    spaces = lax.axis_size("space")
    rank = lax.axis_index("tm").astype(jnp.int32)
    total_blocks = blocks * spaces
    first_block = lax.axis_index("space") * blocks - GHOST
    picked = ((neighbours - first_block) % total_blocks).reshape(frames, -1)
    rows = positions.reshape(frames, 3, blocks, BLOCK).transpose(0, 2, 1, 3)
    rows = rows.reshape(frames, blocks, 3 * BLOCK)
    rows = jnp.pad(rows, ((0, 0), (0, 16 - blocks), (0, width - 3 * BLOCK)))
    ranked = rank.reshape(1)
    weights = (edge_in, edge_out, edge_params, coord_weight.reshape(1, width))

    def ring(shift, count):
        return [(i, (i + shift) % count) for i in range(count)]

    def halo(start, size, low):
        part = slice(start, start + size)
        if low:
            spots = jnp.pad(rows[part, blocks - GHOST : blocks], ((0, 0), (2, 0), (0, 0)))
            block = node_feats[part, local_rows - rim :]
        else:
            spots = jnp.pad(rows[part, :GHOST], ((0, 0), (0, 2), (0, 0)))
            block = node_feats[part, :rim]
        payload = jnp.concatenate([block, spots.astype(jnp.bfloat16)], axis=1)
        return lax.ppermute(payload, "space", ring(1 if low else -1, spaces))

    plans = [("low", 0, GHOST, (16, 24, 24))]
    if blocks > 2 * GHOST:
        plans.insert(0, ("own", GHOST, blocks - 2 * GHOST, (64,)))
    plans.append(("high", blocks - GHOST, GHOST, (32, 32)))
    gathered = []
    moves = {}
    for table, first, count, fractions in plans:
        own, sent, shift_rows = [], [[] for _ in range(1, parts)], []
        for start, size in cut(frames, fractions):
            rim_data = None if table == "own" else halo(start, size, table == "low")
            result = edge_call(
                ranked,
                picked,
                node_feats,
                rows,
                rim_data,
                weights,
                table=table,
                first=first,
                count=count,
                start=start,
                frames=size,
                parts=parts,
            )
            own.append(result[0])
            for r in range(1, parts):
                sent[r - 1].append(lax.ppermute(result[r], "tm", ring(r, parts)))
            shift_rows.append(result[parts])
        gathered.append((first, count, own + [x for group in sent for x in group]))
        moves[first] = jnp.concatenate(shift_rows, axis=0)

    moved = jnp.concatenate([moves[key] for key in sorted(moves)], axis=1)
    moved = moved[:, :, : 3 * BLOCK].reshape(frames, blocks, 3, BLOCK).transpose(0, 2, 1, 3)
    new_positions = positions + moved.reshape(frames, 3, local_rows)

    fwd, inv = transforms(rank, parts, frames, spectral.shape[1])
    node_weights = (node_in, node_out, node_bias)
    buffer = None
    for first, count, data in gathered:
        share = count * BLOCK // parts
        unit = math.gcd(share, BLOCK)
        results = spectral_call(data, fwd, inv, spectral, parts)
        for r in range(parts):
            conv = results[r] if r == 0 else lax.ppermute(results[r], "tm", ring(r, parts))
            source = (rank - r) % parts
            spot = ((first * BLOCK + source * share) // unit).astype(jnp.int32).reshape(1)
            buffer = node_call(spot, node_feats, conv, node_weights, buffer, unit)
    return (buffer, new_positions)


def solution(mesh):
    placed = (
        P("tm", "space", None),
        P("tm", None, "space"),
        P("tm", "space", None),
        P(),
        P(),
        P(),
        P(),
        P(),
        P(),
        P(),
        P(),
    )
    return jax.shard_map(
        shards,
        mesh=mesh,
        in_specs=placed,
        out_specs=(P("tm", "space", None), P("tm", None, "space")),
        check_vma=False,
    )
```

time: 967 us -> 559 us (0.58)
  matrix products: 533 us -> 0 us
  Pallas kernels: 0 us -> 491 us
  local copies, waits for them, and re-layouts: 231 us -> 15.9 us
  waiting for transfers between devices: 129 us -> 21.5 us
  other arithmetic: 46.4 us -> 11.1 us
    dot_general x45 -> x0, matrix products: 533 us -> none  [the longest x8 158 us: edge_pass(): jnp.dot(hidden.reshape(-1, feat_width), edge_out, preferred_element_type=...]
    pallas_call x0 -> x15, Pallas kernels: none -> 491 us  [the longest x6 345 us: edge_call(): pl.pallas_call(functools.partial(edge_body, table=table, base=base, first...]
    reshape x11 -> x2, local copies, waits for them, and re-layouts: 155 us -> 1.02 us  [the longest x1 0.69 us: shards(): picked = ((neighbours - first_block) % total_blocks).reshape(frames, -1)]
    all_to_all x2 -> x0, waiting for transfers between devices: 72.8 us -> none  [the longest x1 47.5 us: shards(): lax.all_to_all(mean_msg, 'tm', split_axis=1, concat_axis=0, tiled=True)]
    ppermute x4 -> x14, waiting for transfers between devices: 56.3 us -> 21.5 us  [the longest x3 21.5 us: shards(): lax.ppermute(results[r], 'tm', ring(r, parts))]
    convert_element_type x1 -> x2, other arithmetic: 29.6 us -> 0.09 us  [split_parts(): low_part = (values - high_part.astype(jnp.float32)).astype(jnp.bfloat16)]
    another operation x1 -> x0, local copies, waits for them, and re-layouts: 28.5 us -> none  [edge_pass(): flat_dst = other_dst.reshape(frames, other_blocks, block_len * feat_width)]
    unnamed x136 -> x28, local copies, waits for them, and re-layouts: 23.7 us -> 5.98 us
  transfers between devices with their start and end apart: 6 -> 14, of which waited for: 4 -> 1; matrix products, arithmetic and copies ran while one was open for 6% -> 3% of each run, Pallas kernels for 0% -> 87%
where the time goes in v1:
time: 559 us; the launch traced here: 556 us
  Pallas kernels  491 us (88%)
  waiting for transfers between devices  21.5 us (4%)
  local copies, waits for them, and re-layouts  15.9 us (3%)
  starting transfers between devices  14.9 us (3%)
  other arithmetic  11.1 us (2%)
    pallas_call x6, Pallas kernels, edge_call(): pl.pallas_call(functools.partial(edge_body, table=table, base=base, first...  345 us
    pallas_call x3, Pallas kernels, spectral_call(): pl.pallas_call(functools.partial(spectral_body, pieces=len(data), parts=p...  97.1 us
    pallas_call x6, Pallas kernels, node_call(): pl.pallas_call(node_body, out_shape=jax.ShapeDtypeStruct(feats.shape, jnp...  49.5 us
    ppermute x3, waiting for transfers between devices, shards(): lax.ppermute(results[r], 'tm', ring(r, parts))  21.5 us
  transfers between devices with their start and end apart: 14, of which 1 were waited for; matrix products, arithmetic and copies ran while one was open for 3% of the time, Pallas kernels for 87%

profile of v1, /device:TPU:1, one launch (start us, length us, event | category | flops | bytes accessed | tf_op | source)
XLA Modules:
  0.0 555.7 jit_solution(6768313887272584164)
XLA Ops:
  0.6 1.2 copy.21
  2.3 1.8 fusion.31
  4.1 1.2 fusion.8
  5.3 2.6 collective-permute-start.7
  8.0 1.2 slice.42
  9.3 1.0 fusion.9
  10.2 1.6 collective-permute-start.5
  11.9 0.8 pad.27.refs_1_
  12.8 0.7 copy.24.picked
  13.5 62.8 %edge_own.1 = (bf16[32,64,128]{2,1,0:T(8,128)(2,1)}, bf16[32,64,128]{2,1,0:T(8,128)(2,1)}, f32[64,2,128]{2,1,0:T(2,128)}) custom-call(s32[64,112]{1,0:T(8,128)} %copy.24.picked, s32[1]{0:T(128)} %bitcast.2.rank, bf16[64,448,128]{2,1,0:T(8,128)(2,1)} %refs_0_.23, f32[64,16,128]{2,1,0:T(8,128)} %pad.27.refs_1_, bf16[256,128]{1,0:T(8,128)(2,1)} %refs_2_.7, ...), custom_call_target="tpu_custom_call" | custom-call | flops 8589934592 | bytes 524288 | tf_op jit(solution)/shard_map/edge_own/pallas_call | solution.py:159
  76.2 1.2 collective-permute-start.12
  77.5 2.1 fusion.32
  79.6 1.3 fusion.5
  80.9 0.5 fusion.26
  81.9 0.6 iota_add_fusion
  82.5 1.3 add.180
  83.8 1.3 iota_add_fusion.1
  85.1 1.3 add.173
  86.3 0.8 cosine_bitcast_fusion
  87.1 0.9 multiply_bitcast_fusion.1
  88.3 0.6 pad_maximum_fusion.7.refs_5_.refs_7_.refs_3_
  88.9 0.6 pad_maximum_fusion.5.refs_4_.refs_6_.refs_2_
  89.6 1.3 fusion.4
  90.8 3.3 collective-permute-start
  94.1 36.5 %edge_low.3 = (bf16[96,16,128]{2,1,0:T(8,128)(2,1)}, bf16[96,16,128]{2,1,0:T(8,128)(2,1)}, f32[16,6,128]{2,1,0:T(8,128)}) custom-call(s32[64,112]{1,0:T(8,128)} %copy.24.picked, s32[1]{0:T(128)} %bitcast.2.rank, bf16[64,448,128]{2,1,0:T(8,128)(2,1)} %refs_0_.23, f32[64,16,128]{2,1,0:T(8,128)} %pad.27.refs_1_, ...), custom_call_target="tpu_custom_call" | custom-call | flops 6442450944 | bytes 393216 | tf_op jit(solution)/shard_map/edge_low/pallas_call | solution.py:159
  130.9 53.2 %edge_low.5 = (bf16[96,24,128]{2,1,0:T(8,128)(2,1)}, bf16[96,24,128]{2,1,0:T(8,128)(2,1)}, f32[24,6,128]{2,1,0:T(8,128)}) custom-call(s32[64,112]{1,0:T(8,128)} %copy.24.picked, s32[1]{0:T(128)} %bitcast.2.rank, bf16[64,448,128]{2,1,0:T(8,128)(2,1)} %refs_0_.23, f32[64,16,128]{2,1,0:T(8,128)} %pad.27.refs_1_, ...), custom_call_target="tpu_custom_call" | custom-call | flops 9663676416 | bytes 589824 | tf_op jit(solution)/shard_map/edge_low/pallas_call | solution.py:159
  184.2 1.3 collective-permute-start.10
  185.5 53.3 %edge_low.4 = (bf16[96,24,128]{2,1,0:T(8,128)(2,1)}, bf16[96,24,128]{2,1,0:T(8,128)(2,1)}, f32[24,6,128]{2,1,0:T(8,128)}) custom-call(s32[64,112]{1,0:T(8,128)} %copy.24.picked, s32[1]{0:T(128)} %bitcast.2.rank, bf16[64,448,128]{2,1,0:T(8,128)(2,1)} %refs_0_.23, f32[64,16,128]{2,1,0:T(8,128)} %pad.27.refs_1_, ...), custom_call_target="tpu_custom_call" | custom-call | flops 9663676416 | bytes 589824 | tf_op jit(solution)/shard_map/edge_low/pallas_call | solution.py:159
  239.1 69.5 %edge_high.3 = (bf16[96,32,128]{2,1,0:T(8,128)(2,1)}, bf16[96,32,128]{2,1,0:T(8,128)(2,1)}, f32[32,6,128]{2,1,0:T(8,128)}) custom-call(s32[64,112]{1,0:T(8,128)} %copy.24.picked, s32[1]{0:T(128)} %bitcast.2.rank, bf16[64,448,128]{2,1,0:T(8,128)(2,1)} %refs_0_.23, f32[64,16,128]{2,1,0:T(8,128)} %pad.27.refs_1_, ...), custom_call_target="tpu_custom_call" | custom-call | flops 12884901888 | bytes 786432 | tf_op jit(solution)/shard_map/edge_high/pallas_call | solution.py:159
  308.6 1.3 collective-permute-start.3
  309.9 69.4 %edge_high.2 = (bf16[96,32,128]{2,1,0:T(8,128)(2,1)}, bf16[96,32,128]{2,1,0:T(8,128)(2,1)}, f32[32,6,128]{2,1,0:T(8,128)}) custom-call(s32[64,112]{1,0:T(8,128)} %copy.24.picked, s32[1]{0:T(128)} %bitcast.2.rank, bf16[64,448,128]{2,1,0:T(8,128)(2,1)} %refs_0_.23, f32[64,16,128]{2,1,0:T(8,128)} %pad.27.refs_1_, ...), custom_call_target="tpu_custom_call" | custom-call | flops 12884901888 | bytes 786432 | tf_op jit(solution)/shard_map/edge_high/pallas_call | solution.py:159
  379.4 0.7 copy-done.12
  380.3 0.8 copy-done.10
  381.4 39.4 %spectral.4 = (bf16[64,96,128]{2,1,0:T(8,128)(2,1)}, bf16[64,96,128]{2,1,0:T(8,128)(2,1)}) custom-call(bf16[96,16,128]{2,1,0:T(8,128)(2,1)} %get-tuple-element.32.refs_0_, bf16[96,24,128]{2,1,0:T(8,128)(2,1)} %get-tuple-element.33.refs_1_, bf16[96,24,128]{2,1,0:T(8,128)(2,1)} %get-tuple-element.34.refs_2_, bf16[96,16,128]{2,1,0:T(8,128)(2,1)} %copy-done.12, ...), custom_call_target="tpu_custom_call" | custom-call | flops 11274289152 | bytes 6291456 | tf_op jit(solution)/shard_map/spectral/pallas_call | solution.py:251
  420.8 1.2 collective-permute-start.11
  422.0 0.9 copy-done.8
  423.2 39.5 %spectral.3 = (bf16[64,96,128]{2,1,0:T(8,128)(2,1)}, bf16[64,96,128]{2,1,0:T(8,128)(2,1)}) custom-call(bf16[96,32,128]{2,1,0:T(8,128)(2,1)} %get-tuple-element.26.refs_0_, bf16[96,32,128]{2,1,0:T(8,128)(2,1)} %get-tuple-element.27.refs_1_, bf16[96,32,128]{2,1,0:T(8,128)(2,1)} %copy-done.9, bf16[96,32,128]{2,1,0:T(8,128)(2,1)} %copy-done.8, ...), custom_call_target="tpu_custom_call" | custom-call | flops 11274289152 | bytes 6291456 | tf_op jit(solution)/shard_map/spectral/pallas_call | solution.py:251
  462.9 18.2 %spectral.5 = (bf16[64,32,128]{2,1,0:T(8,128)(2,1)}, bf16[64,32,128]{2,1,0:T(8,128)(2,1)}) custom-call(bf16[32,64,128]{2,1,0:T(8,128)(2,1)} %get-tuple-element.40.refs_0_, bf16[32,64,128]{2,1,0:T(8,128)(2,1)} %collective-permute-done.12.refs_1_, bf16[2,128,128]{2,1,0:T(8,128)(2,1)} %pad_maximum_fusion.5.refs_4_.refs_6_.refs_2_, ...), custom_call_target="tpu_custom_call" | custom-call | flops 3758096384 | bytes 2097152 | tf_op jit(solution)/shard_map/spectral/pallas_call | solution.py:251
  481.1 1.2 collective-permute-start.13
  482.3 4.6 node.6.refs_5_
  487.0 21.5 %collective-permute-done.13.refs_1_ = bf16[64,32,128]{2,1,0:T(8,128)(2,1)S(1)} collective-permute-done((bf16[64,32,128]{2,1,0:T(8,128)(2,1)}, bf16[64,32,128]{2,1,0:T(8,128)(2,1)S(1)}, u32[]{:S(2)}, u32[]{:S(2)}) %collective-permute-start.13) | collective-permute-done | bytes 524320 | tf_op jit(solution)/shard_map/ppermute | solution.py:440
  508.4 0.8 copy-done
  509.3 4.7 node.7.refs_5_
  514.5 1.0 copy.33
  515.5 10.0 %node.8.refs_5_ = bf16[64,448,128]{2,1,0:T(8,128)(2,1)} custom-call(s32[1]{0:T(128)} %bitcast.13.spot, bf16[64,448,128]{2,1,0:T(8,128)(2,1)} %refs_0_.23, bf16[64,96,128]{2,1,0:T(8,128)(2,1)} %get-tuple-element.39.refs_1_, bf16[256,128]{1,0:T(8,128)(2,1)} %refs_2_.13, bf16[128,128]{1,0:T(8,128)(2,1)} %refs_3_.23, ...), custom_call_target="tpu_custom_call", output_to_operand_aliasing={{}: (6, {})} | custom-call | flops 1207959552 | bytes 4718592 | tf_op jit(solution)/shard_map/node/pallas_call | solution.py:307
  525.6 10.1 %node.9.refs_5_ = bf16[64,448,128]{2,1,0:T(8,128)(2,1)} custom-call(s32[1]{0:T(128)} %bitcast.12.spot, bf16[64,448,128]{2,1,0:T(8,128)(2,1)} %refs_0_.23, bf16[64,96,128]{2,1,0:T(8,128)(2,1)} %collective-permute-done.11.refs_1_, bf16[256,128]{1,0:T(8,128)(2,1)} %refs_2_.13, bf16[128,128]{1,0:T(8,128)(2,1)} %refs_3_.23, ...), custom_call_target="tpu_custom_call", output_to_operand_aliasing={{}: (6, {})} | custom-call | flops 1207959552 | bytes 4718592 | tf_op jit(solution)/shard_map/node/pallas_call | solution.py:307
  535.6 10.1 %node.10.refs_5_ = bf16[64,448,128]{2,1,0:T(8,128)(2,1)} custom-call(s32[1]{0:T(128)} %bitcast.11.spot, bf16[64,448,128]{2,1,0:T(8,128)(2,1)} %refs_0_.23, bf16[64,96,128]{2,1,0:T(8,128)(2,1)} %get-tuple-element.31.refs_1_, bf16[256,128]{1,0:T(8,128)(2,1)} %refs_2_.13, bf16[128,128]{1,0:T(8,128)(2,1)} %refs_3_.23, ...), custom_call_target="tpu_custom_call", output_to_operand_aliasing={{}: (6, {})} | custom-call | flops 1207959552 | bytes 4718592 | tf_op jit(solution)/shard_map/node/pallas_call | solution.py:307
  545.7 10.1 %node.11 = bf16[64,448,128]{2,1,0:T(8,128)(2,1)} custom-call(s32[1]{0:T(128)} %bitcast.spot, bf16[64,448,128]{2,1,0:T(8,128)(2,1)} %refs_0_.23, bf16[64,96,128]{2,1,0:T(8,128)(2,1)} %collective-permute-done.4.refs_1_, bf16[256,128]{1,0:T(8,128)(2,1)} %refs_2_.13, bf16[128,128]{1,0:T(8,128)(2,1)} %refs_3_.23, ...), custom_call_target="tpu_custom_call", output_to_operand_aliasing={{}: (6, {})} | custom-call | flops 1207959552 | bytes 4718592 | tf_op jit(solution)/shard_map/node/pallas_call | solution.py:307
  (57 shorter events, 3.3 us)
Async XLA Ops:
  5.3 125.4 %collective-permute-start.7 = (bf16[24,200,128]{2,1,0:T(8,128)(2,1)}, bf16[24,200,128]{2,1,0:T(8,128)(2,1)}, u32[]{:S(2)}, u32[]{:S(2)}) collective-permute-start(bf16[24,200,128]{2,1,0:T(8,128)(2,1)} %fusion.8), channel_id=1, source_target_pairs={{0,2},{2,4},{4,6},{6,8},{8,10},{10,12},{12,14},{14,16},{16,18},{18... | collective-permute-start | bytes 3686408 | tf_op jit(solution)/shard_map/ppermute | solution.py:395
  8.0 176.2 %collective-permute-start.6 = (bf16[24,200,128]{2,1,0:T(8,128)(2,1)S(1)}, bf16[24,200,128]{2,1,0:T(8,128)(2,1)}, u32[]{:S(2)}, u32[]{:S(2)}) collective-permute-start(bf16[24,200,128]{2,1,0:T(8,128)(2,1)S(1)} %fusion.7), channel_id=1, source_target_pairs={{0,2},{2,4},{4,6},{6,8},{8,10},{10,12},{12,14},{14,16},{16,18},{18... | collective-permute-start | bytes 3686408 | tf_op jit(solution)/shard_map/ppermute | solution.py:395
  9.2 3.5 copy-start.7
  10.2 80.6 %collective-permute-start.5 = (bf16[16,200,128]{2,1,0:T(8,128)(2,1)}, bf16[16,200,128]{2,1,0:T(8,128)(2,1)}, u32[]{:S(2)}, u32[]{:S(2)}) collective-permute-start(bf16[16,200,128]{2,1,0:T(8,128)(2,1)} %fusion.9), channel_id=1, source_target_pairs={{0,2},{2,4},{4,6},{6,8},{8,10},{10,12},{12,14},{14,16},{16,18},{18... | collective-permute-start | bytes 2457608 | tf_op jit(solution)/shard_map/ppermute | solution.py:395
  76.2 386.7 %collective-permute-start.12 = (bf16[32,64,128]{2,1,0:T(8,128)(2,1)}, bf16[32,64,128]{2,1,0:T(8,128)(2,1)}, u32[]{:S(2)}, u32[]{:S(2)}) collective-permute-start(bf16[32,64,128]{2,1,0:T(8,128)(2,1)} %get-tuple-element.41), channel_id=1, source_target_pairs={{0,1},{1,0},{2,3},{3,2},{4,5},{5,4},{6,7},{7,6},{8,9},{9,8},{10,11... | collective-permute-start | bytes 1572872 | tf_op jit(solution)/shard_map/ppermute | solution.py:423
  80.9 157.9 %collective-permute-start.1 = (bf16[32,200,128]{2,1,0:T(8,128)(2,1)}, bf16[32,200,128]{2,1,0:T(8,128)(2,1)}, u32[]{:S(2)}, u32[]{:S(2)}) collective-permute-start(bf16[32,200,128]{2,1,0:T(8,128)(2,1)} %fusion.5), channel_id=1, source_target_pairs={{0,30},{2,0},{4,2},{6,4},{8,6},{10,8},{12,10},{14,12},{16,14},{18,... | collective-permute-start | bytes 4915208 | tf_op jit(solution)/shard_map/ppermute | solution.py:395
  90.8 217.7 %collective-permute-start = (bf16[32,200,128]{2,1,0:T(8,128)(2,1)}, bf16[32,200,128]{2,1,0:T(8,128)(2,1)}, u32[]{:S(2)}, u32[]{:S(2)}) collective-permute-start(bf16[32,200,128]{2,1,0:T(8,128)(2,1)} %fusion.4), channel_id=1, source_target_pairs={{0,30},{2,0},{4,2},{6,4},{8,6},{10,8},{12,10},{14,12},{16,14},{18,... | collective-permute-start | bytes 4915208 | tf_op jit(solution)/shard_map/ppermute | solution.py:395
  130.7 248.7 %collective-permute-start.8 = (bf16[96,16,128]{2,1,0:T(8,128)(2,1)}, bf16[96,16,128]{2,1,0:T(8,128)(2,1)S(1)}, u32[]{:S(2)}, u32[]{:S(2)}) collective-permute-start(bf16[96,16,128]{2,1,0:T(8,128)(2,1)} %get-tuple-element.35), channel_id=1, source_target_pairs={{0,1},{1,0},{2,3},{3,2},{4,5},{5,4},{6,7},{7,6},{8,9},{9,8},{10,11... | collective-permute-start | bytes 1179656 | tf_op jit(solution)/shard_map/ppermute | solution.py:423
  184.2 196.1 %collective-permute-start.10 = (bf16[96,24,128]{2,1,0:T(8,128)(2,1)}, bf16[96,24,128]{2,1,0:T(8,128)(2,1)S(1)}, u32[]{:S(2)}, u32[]{:S(2)}) collective-permute-start(bf16[96,24,128]{2,1,0:T(8,128)(2,1)} %get-tuple-element.37), channel_id=1, source_target_pairs={{0,1},{1,0},{2,3},{3,2},{4,5},{5,4},{6,7},{7,6},{8,9},{9,8},{10,11... | collective-permute-start | bytes 1769480 | tf_op jit(solution)/shard_map/ppermute | solution.py:423
  238.8 141.5 %collective-permute-start.9 = (bf16[96,24,128]{2,1,0:T(8,128)(2,1)}, bf16[96,24,128]{2,1,0:T(8,128)(2,1)S(1)}, u32[]{:S(2)}, u32[]{:S(2)}) collective-permute-start(bf16[96,24,128]{2,1,0:T(8,128)(2,1)} %get-tuple-element.36), channel_id=1, source_target_pairs={{0,1},{1,0},{2,3},{3,2},{4,5},{5,4},{6,7},{7,6},{8,9},{9,8},{10,11... | collective-permute-start | bytes 1769480 | tf_op jit(solution)/shard_map/ppermute | solution.py:423
  308.6 113.4 %collective-permute-start.3 = (bf16[96,32,128]{2,1,0:T(8,128)(2,1)}, bf16[96,32,128]{2,1,0:T(8,128)(2,1)S(1)}, u32[]{:S(2)}, u32[]{:S(2)}) collective-permute-start(bf16[96,32,128]{2,1,0:T(8,128)(2,1)} %get-tuple-element.29), channel_id=1, source_target_pairs={{0,1},{1,0},{2,3},{3,2},{4,5},{5,4},{6,7},{7,6},{8,9},{9,8},{10,11... | collective-permute-start | bytes 2359304 | tf_op jit(solution)/shard_map/ppermute | solution.py:423
  379.3 0.8 copy-start.12
  380.1 41.9 %collective-permute-start.2 = (bf16[96,32,128]{2,1,0:T(8,128)(2,1)}, bf16[96,32,128]{2,1,0:T(8,128)(2,1)S(1)}, u32[]{:S(2)}, u32[]{:S(2)}) collective-permute-start(bf16[96,32,128]{2,1,0:T(8,128)(2,1)} %get-tuple-element.28), channel_id=1, source_target_pairs={{0,1},{1,0},{2,3},{3,2},{4,5},{5,4},{6,7},{7,6},{8,9},{9,8},{10,11... | collective-permute-start | bytes 2359304 | tf_op jit(solution)/shard_map/ppermute | solution.py:423
  380.3 0.8 copy-start.10
  380.3 1.0 copy-start.11
  420.8 104.8 %collective-permute-start.11 = (bf16[64,96,128]{2,1,0:T(8,128)(2,1)}, bf16[64,96,128]{2,1,0:T(8,128)(2,1)}, u32[]{:S(2)}, u32[]{:S(2)}) collective-permute-start(bf16[64,96,128]{2,1,0:T(8,128)(2,1)} %get-tuple-element.38), channel_id=1, source_target_pairs={{0,1},{1,0},{2,3},{3,2},{4,5},{5,4},{6,7},{7,6},{8,9},{9,8},{10,11... | collective-permute-start | bytes 4718600 | tf_op jit(solution)/shard_map/ppermute | solution.py:440
  422.0 0.9 copy-start.8
  422.0 1.2 copy-start.9
  462.7 83.0 %collective-permute-start.4 = (bf16[64,96,128]{2,1,0:T(8,128)(2,1)}, bf16[64,96,128]{2,1,0:T(8,128)(2,1)}, u32[]{:S(2)}, u32[]{:S(2)}) collective-permute-start(bf16[64,96,128]{2,1,0:T(8,128)(2,1)} %get-tuple-element.30), channel_id=1, source_target_pairs={{0,1},{1,0},{2,3},{3,2},{4,5},{5,4},{6,7},{7,6},{8,9},{9,8},{10,11... | collective-permute-start | bytes 4718600 | tf_op jit(solution)/shard_map/ppermute | solution.py:440
  481.1 27.4 %collective-permute-start.13 = (bf16[64,32,128]{2,1,0:T(8,128)(2,1)}, bf16[64,32,128]{2,1,0:T(8,128)(2,1)S(1)}, u32[]{:S(2)}, u32[]{:S(2)}) collective-permute-start(bf16[64,32,128]{2,1,0:T(8,128)(2,1)} %get-tuple-element.42), channel_id=1, source_target_pairs={{0,1},{1,0},{2,3},{3,2},{4,5},{5,4},{6,7},{7,6},{8,9},{9,8},{10,11... | collective-permute-start | bytes 1572872 | tf_op jit(solution)/shard_map/ppermute | solution.py:440
  508.4 0.8 copy-start
  509.2 4.7 copy-start.1
  509.2 4.7 copy-start.2
  509.2 4.7 copy-start.3
  509.2 4.8 copy-start.4
  509.3 4.8 copy-start.5
  509.3 4.8 copy-start.6
